TPU v7x, 256 devices: a whole 4x4x8 slice. The times are simulated.
256 devices in a mesh: seq: 128 (over x, z, y), mp: 2 (over core).
Axes of the slice: x: 4, y: 4, z: 8, core: 2. Of those that a mesh axis runs over, the one named last changes fastest.
Arguments:
- states: bfloat16 [32768, 768], P('seq'), may hold values from -24 to 24
- qkv_weight: bfloat16 [3, 768, 768], P(None, None, 'mp'), may hold values from -0.21875 to 0.21875
- out_weight: bfloat16 [768, 768], P('mp'), may hold values from -0.21875 to 0.21875
- up_weight: bfloat16 [768, 3072], P(None, 'mp'), may hold values from -0.21875 to 0.21875
- down_weight: bfloat16 [3072, 768], P('mp'), may hold values from -0.109375 to 0.109375
- attn_gain: float32 [768], replicated, may hold values from 0.5 to 1.5
- mlp_gain: float32 [768], replicated, may hold values from 0.5 to 1.5
- global_ids: int32 [2], replicated, may hold values from 0 to 511, as said below
- random_owner: int32 [2, 512, 6, 3], P('mp', 'seq'), may hold values from 0 to 127, all different within a row; in each aligned block of 24 rows (0 to 23, 24 to 47, ..., all dimensions but the last counted through in order) at most 2 rows name the same one
- random_local: int32 [2, 512, 6, 3], P('mp', 'seq'), may hold values from 0 to 3
Outputs:
- layer_out: bfloat16 [32768, 768], P('seq')
Inputs may be any that keep to these rules, and one draw needn't show every extreme that they name: `global_ids`: 2 different block numbers; the second is 511. The random key block is random_owner * 4 + random_local. For one query block and head the 3 owners differ. Within the rows of one device (aligned blocks of 4 * K rows over the first three dimensions, K the third dimension) no owner is named more than 2 times, a bound that some block reaches.
All inputs are finite; a program needn't handle non-finite values.
Results may differ from a plain program's by a relative error of at most 0.008.
The roundings to bfloat16 on the way count: a program that leaves them out, or rounds other values in their place, can miss the bound.
Values may be sent and summed in bfloat16 or wider, within the bound.
No kernel may reach another device: no remote copies, remote signals or barrier semaphores. Data moves between devices by JAX's collectives and lax.ppermute only.
A program may use at most 192 MiB of HBM per device.

v0:
```python
import jax
import jax.numpy as jnp
from jax import lax
from jax.sharding import Mesh
from jax.sharding import PartitionSpec as P

HD = 64
BS = 64
R = 3
G = 2
SEQ = ("seq_0", "seq_1", "seq_2")
EPSILON = 1e-05
NEGATIVE = -1e30


def from_root(value, axes, root):
    value = jnp.where(lax.axis_index(axes) == root, value, jnp.zeros_like(value))
    for axis in axes:
        value = lax.psum(value, axis)
    return value


def with_halo(cells, sides, width):
    for axis, dim in sides:
        count = lax.axis_size(axis)
        ends = count - 1
        head = lax.slice_in_dim(cells, 0, width, axis=dim)
        tail = lax.slice_in_dim(cells, cells.shape[dim] - width, cells.shape[dim], axis=dim)
        cells = jnp.concatenate(
            [
                lax.ppermute(tail, axis, [(i, (i + 1) % count) for i in range(ends)]),
                cells,
                lax.ppermute(head, axis, [((i + 1) % count, i) for i in range(ends)]),
            ],
            axis=dim,
        )
    return cells


def collected_together(value, axis):
    leaves = jax.tree.leaves(value)
    order = sorted(range(len(leaves)), key=lambda k: -leaves[k].size)
    width = (1, *leaves[order[0]].shape)[-1]
    lines = [
        jnp.pad(leaves[k].reshape(-1), (0, -leaves[k].size % width)).reshape(-1, width)
        for k in order
    ]
    both, at, found = (lax.all_gather(jnp.concatenate(lines), axis), 0, {})
    for k, line in zip(order, lines):
        share = both[:, at : at + len(line)].reshape(len(both), -1)
        found[k] = share[:, : leaves[k].size].reshape(-1, *leaves[k].shape)
        at += len(line)
    numbers = iter(range(len(leaves)))
    return jax.tree.map(lambda _: found[next(numbers)], value)


def joined_all(value, axes, combine):
    for axis in axes:
        pieces = collected_together(value, axis)
        value = jax.tree.map(lambda part: part[0], pieces)
        for k in range(1, lax.axis_size(axis)):
            value = combine(value, jax.tree.map(lambda part: part[k], pieces))
    return value


def from_everyone(value, axis):
    copies = jnp.broadcast_to(value, (lax.axis_size(axis), *value.shape))
    return lax.all_to_all(copies, axis, split_axis=0, concat_axis=0, tiled=True)


def taken_together(value, axis):
    return from_everyone(value, axis).sum(axis=0)


def layer_norm(inputs, scales):
    center = jnp.mean(inputs, axis=-1, keepdims=True)
    shifted = inputs - center
    spread = jnp.mean(shifted * shifted, axis=-1, keepdims=True)
    return shifted * lax.rsqrt(spread + EPSILON) * scales


def merge_partials(earlier, later):
    high_early, total_early, acc_early = earlier
    high_late, total_late, acc_late = later
    highest = jnp.maximum(high_early, high_late)
    factor_early = jnp.exp(high_early - highest)
    factor_late = jnp.exp(high_late - highest)
    total = total_early * factor_early + total_late * factor_late
    summed = acc_early * factor_early[..., None] + acc_late * factor_late[..., None]
    return (highest, total, summed)


def fetch_global(query_blocks, pair_blocks, owner, local_block):
    query_piece = lax.dynamic_index_in_dim(query_blocks, local_block, 0, keepdims=False)
    pair_piece = lax.dynamic_index_in_dim(pair_blocks, local_block, 0, keepdims=False)
    return (from_root(query_piece, SEQ, owner), from_root(pair_piece, SEQ, owner))


def shards(
    states,
    qkv_weight,
    out_weight,
    up_weight,
    down_weight,
    attn_gain,
    mlp_gain,
    global_ids,
    random_owner,
    random_local,
):
    tokens_here = states.shape[0]
    head_width = qkv_weight.shape[2]
    head_count = head_width // HD
    block_count = tokens_here // BS
    seq_count = lax.axis_size(SEQ)
    position = lax.axis_index(SEQ)
    first_block = position * block_count
    scaling = HD ** (-0.5)
    highest = lax.Precision.HIGHEST
    queries = jnp.dot(states, qkv_weight[0], preferred_element_type=jnp.float32).astype(
        jnp.bfloat16
    )
    query_blocks = queries.reshape(block_count, BS, head_count, HD)
    key_part = jnp.dot(states, qkv_weight[1], preferred_element_type=jnp.float32).astype(
        jnp.bfloat16
    )
    value_part = jnp.dot(states, qkv_weight[2], preferred_element_type=jnp.float32).astype(
        jnp.bfloat16
    )
    key_value = jnp.concatenate(
        [
            key_part.reshape(tokens_here, head_count, HD),
            value_part.reshape(tokens_here, head_count, HD),
        ],
        axis=2,
    )
    pair_blocks = key_value.reshape(block_count, BS, head_count, 2 * HD)
    owner_of = global_ids // block_count
    local_of = global_ids % block_count
    fetched = [
        fetch_global(query_blocks, pair_blocks, owner_of[number], local_of[number])
        for number in range(G)
    ]
    global_query = jnp.stack([item[0] for item in fetched])
    global_pair = jnp.stack([item[1] for item in fetched])
    padded = with_halo(key_value, ((SEQ, 0),), BS)
    padded = padded.reshape(block_count + 2, BS, head_count, 2 * HD)
    window = jnp.stack([padded[shift_by : shift_by + block_count] for shift_by in range(3)], axis=1)
    neighbour = (
        first_block
        + jnp.arange(block_count, dtype=jnp.int32)[:, None]
        + jnp.arange(-1, 2, dtype=jnp.int32)[None, :]
    )
    inside = (neighbour >= 0) & (neighbour < seq_count * block_count)
    score_window = (
        jnp.einsum(
            "bqhd,bwkhd->bhqwk", query_blocks, window[..., :HD], preferred_element_type=jnp.float32
        )
        * scaling
    )
    score_window = jnp.where(inside[:, None, None, :, None], score_window, NEGATIVE)
    score_global = (
        jnp.einsum(
            "bqhd,gkhd->bhqgk",
            query_blocks,
            global_pair[..., :HD],
            preferred_element_type=jnp.float32,
        )
        * scaling
    )
    owner_list = random_owner.reshape(-1)
    local_list = random_local.reshape(-1)
    item_count = owner_list.shape[0]
    capacity = max(2, item_count // seq_count + 1)
    slot_total = seq_count * capacity
    head_list = jnp.broadcast_to(
        jnp.arange(head_count, dtype=jnp.int32)[None, :, None], (block_count, head_count, R)
    ).reshape(-1)
    matches = (owner_list[:, None] == jnp.arange(seq_count, dtype=jnp.int32)[None, :]).astype(
        jnp.int32
    )
    slot_rank = jnp.sum((jnp.cumsum(matches, axis=0) - matches) * matches, axis=1)
    slot_index = owner_list * capacity + slot_rank
    block_table = pair_blocks.transpose(0, 2, 1, 3).reshape(block_count * head_count, BS, 2 * HD)
    wanted = (
        jnp.zeros((slot_total,), jnp.int32).at[slot_index].set(local_list * head_count + head_list)
    )
    wanted = wanted.reshape(seq_count, capacity)
    remote = lax.all_to_all(
        block_table[lax.all_to_all(wanted, SEQ, split_axis=0, concat_axis=0, tiled=True)],
        SEQ,
        split_axis=0,
        concat_axis=0,
        tiled=True,
    ).reshape(slot_total, BS, 2 * HD)[slot_index]
    remote = remote.reshape(block_count, head_count, R, BS, 2 * HD)
    score_random = (
        jnp.einsum(
            "bqhd,bhrkd->bhqrk", query_blocks, remote[..., :HD], preferred_element_type=jnp.float32
        )
        * scaling
    )
    joined = jnp.concatenate([score_window, score_random, score_global], axis=3)
    joined_shape = joined.shape
    flat_scores = joined.reshape(joined_shape[0], joined_shape[1], joined_shape[2], -1)
    row_high = jnp.max(flat_scores, axis=-1, keepdims=True)
    raised = jnp.exp(flat_scores - row_high)
    weights = (
        (raised / jnp.sum(raised, axis=-1, keepdims=True))
        .astype(jnp.bfloat16)
        .reshape(joined_shape)
    )
    mixed = jnp.einsum(
        "bhqwk,bwkhd->bqhd",
        weights[:, :, :, :3],
        window[..., HD:],
        preferred_element_type=jnp.float32,
    )
    mixed = mixed + jnp.einsum(
        "bhqrk,bhrkd->bqhd",
        weights[:, :, :, 3 : 3 + R],
        remote[..., HD:],
        preferred_element_type=jnp.float32,
    )
    mixed = mixed + jnp.einsum(
        "bhqgk,gkhd->bqhd",
        weights[:, :, :, 3 + R :],
        global_pair[..., HD:],
        preferred_element_type=jnp.float32,
    )
    global_scores = (
        jnp.einsum(
            "gqhd,khd->hgqk",
            global_query,
            key_part.reshape(tokens_here, head_count, HD),
            preferred_element_type=jnp.float32,
        )
        * scaling
    )
    local_high = jnp.max(global_scores, axis=-1)
    global_raised = jnp.exp(global_scores - local_high[..., None])
    local_total = jnp.sum(global_raised, axis=-1)
    local_acc = jnp.einsum(
        "hgqk,khd->hgqd",
        global_raised,
        value_part.reshape(tokens_here, head_count, HD).astype(jnp.float32),
        precision=highest,
    )
    merged_high, merged_total, merged_acc = joined_all(
        (local_high, local_total, local_acc), SEQ, merge_partials
    )
    global_out = merged_acc / merged_total[..., None]
    placed_here = (
        global_ids[:, None] == first_block + jnp.arange(block_count, dtype=jnp.int32)[None, :]
    ).astype(jnp.float32)
    keep_rows = 1.0 - jnp.sum(placed_here, axis=0)
    placed = jnp.einsum("gb,hgqd->bqhd", placed_here, global_out, precision=highest)
    attended = (
        (mixed * keep_rows[:, None, None, None] + placed)
        .astype(jnp.bfloat16)
        .reshape(tokens_here, head_width)
    )
    projected = taken_together(
        jnp.dot(attended, out_weight, preferred_element_type=jnp.float32), "mp"
    )
    normed = layer_norm(states.astype(jnp.float32) + projected, attn_gain).astype(jnp.bfloat16)
    hidden = jax.nn.gelu(
        jnp.dot(normed, up_weight, preferred_element_type=jnp.float32), approximate=False
    ).astype(jnp.bfloat16)
    expanded = taken_together(
        jnp.dot(hidden, down_weight, preferred_element_type=jnp.float32), "mp"
    )
    return layer_norm(normed.astype(jnp.float32) + expanded, mlp_gain).astype(jnp.bfloat16)


def solution(mesh):
    split = Mesh(mesh.devices.reshape(4, 8, 4, mesh.shape["mp"]), ("seq_0", "seq_1", "seq_2", "mp"))
    placed = (
        P(SEQ, None),
        P(None, None, "mp"),
        P("mp", None),
        P(None, "mp"),
        P("mp", None),
        P(),
        P(),
        P(),
        P("mp", SEQ, None, None),
        P("mp", SEQ, None, None),
    )
    return jax.shard_map(
        shards, mesh=split, in_specs=placed, out_specs=P(SEQ, None), check_vma=False
    )
```

profile of v0, /device:TPU:1, one launch (start us, length us, event | category | flops | bytes accessed | tf_op | source)
XLA Modules:
  0.0 507.3 jit_solution(957818700047756081)
XLA Ops:
  11.5 16.9 %all-to-all-start = ((s32[128,1,2]{2,1,0:T(1,128)}), s32[128,1,2]{2,1,0:T(1,128)}, u32[]{:S(2)}, u32[]{:S(2)}) async-start(s32[128,1,2]{2,1,0:T(1,128)} %bitcast.15), calls=%async_computation | async-start | bytes 131072 | tf_op jit(solution)/shard_map/all_to_all | solution.py:190
  38.2 2.1 convolution_convert_fusion.2
  40.3 2.1 convolution_convert_fusion.1
  42.4 2.0 reshape.968
  45.6 2.1 reshape.969
  48.8 35.2 %all-reduce.21.cloned.1.call-done = (bf16[64,6,64]{2,0,1:T(8,128)(2,1)}, bf16[64,6,64]{2,0,1:T(8,128)(2,1)}) async-done(((bf16[64,6,64]{2,0,1:T(8,128)(2,1)}, bf16[64,6,64]{2,0,1:T(8,128)(2,1)}), (bf16[64,6,64]{2,0,1:T(8,128)(2,1)}, bf16[64,6,64]{2,0,1:T(8,128)(2,1)})) %all-reduce.21.cloned.1.call-update) | async-done | bytes 98320 | tf_op jit(solution)/shard_map/psum | solution.py:19
  86.2 70.2 %all-reduce.13.cloned.1.call-done = (bf16[64,6,64]{2,0,1:T(8,128)(2,1)}, bf16[64,6,64]{2,0,1:T(8,128)(2,1)}) async-done(((bf16[64,6,64]{2,0,1:T(8,128)(2,1)}, bf16[64,6,64]{2,0,1:T(8,128)(2,1)}), (bf16[64,6,64]{2,0,1:T(8,128)(2,1)}, bf16[64,6,64]{2,0,1:T(8,128)(2,1)})) %all-reduce.13.cloned.1.call-update) | async-done | bytes 98320 | tf_op jit(solution)/shard_map/psum | solution.py:19
  156.4 3.1 gather_fusion
  159.5 12.3 %all-to-all-start.1 = ((bf16[128,2,64,128]{3,2,1,0:T(8,128)(2,1)}), bf16[128,2,64,128]{3,2,1,0:T(8,128)(2,1)}, u32[]{:S(2)}, u32[]{:S(2)}) async-start(bf16[128,2,64,128]{3,2,1,0:T(8,128)(2,1)} %bitcast.514), calls=%async_computation.1 | async-start | bytes 8388608 | tf_op jit(solution)/shard_map/all_to_all | solution.py:189
  172.9 39.6 %all-reduce.23.cloned.1.call-done = (bf16[64,6,128]{2,0,1:T(8,128)(2,1)}, bf16[64,6,128]{2,0,1:T(8,128)(2,1)}) async-done(((bf16[64,6,128]{2,0,1:T(8,128)(2,1)}, bf16[64,6,128]{2,0,1:T(8,128)(2,1)}), (bf16[64,6,128]{2,0,1:T(8,128)(2,1)}, bf16[64,6,128]{2,0,1:T(8,128)(2,1)})) %all-reduce.23.cloned.1.call-update) | async-done | bytes 196624 | tf_op jit(solution)/shard_map/psum | solution.py:19
  212.6 51.9 %all-reduce.17.cloned.1.call-done = (bf16[1,64,6,64]{3,1,0,2:T(8,128)(2,1)}, bf16[1,64,6,64]{3,1,2,0:T(8,128)(2,1)}) async-done(((bf16[1,64,6,64]{3,1,0,2:T(8,128)(2,1)}, bf16[1,64,6,64]{3,1,2,0:T(8,128)(2,1)}), (bf16[1,64,6,64]{3,1,0,2:T(8,128)(2,1)}, bf16[1,64,6,64]{3,1,2,0:T(8,128)(2,1)})) %all-reduce.17.cloned.1.call-update) | async-done | bytes 98320 | tf_op jit(solution)/shard_map/psum | solution.py:19
  266.3 2.3 fusion.27
  269.9 12.6 %all-gather.3 = f32[4,792,64]{1,2,0:T(8,128)S(1)} all-gather(f32[1,792,64]{1,2,0:T(8,128)S(1)} %maximum_bitcast_fusion), channel_id=2, replica_groups=mesh['seq_0'=4,'seq_1'=8,'seq_2'=4,'mp'=2] {'seq_0'}, dimensions={0}, use_global_device_ids=true | all-gather | bytes 1013760 | tf_op jit(solution)/shard_map/all_gather | solution.py:48
  286.0 50.0 %all-reduce.15.cloned.1.call-done = (bf16[64,6,128]{2,0,1:T(8,128)(2,1)}, bf16[64,6,128]{2,0,1:T(8,128)(2,1)}) async-done(((bf16[64,6,128]{2,0,1:T(8,128)(2,1)}, bf16[64,6,128]{2,0,1:T(8,128)(2,1)}), (bf16[64,6,128]{2,0,1:T(8,128)(2,1)}, bf16[64,6,128]{2,0,1:T(8,128)(2,1)})) %all-reduce.15.cloned.1.call-update) | async-done | bytes 196624 | tf_op jit(solution)/shard_map/psum | solution.py:19
  336.2 1.8 maximum_bitcast_fusion.1
  339.8 3.8 collective-permute-start
  347.6 2.0 copy.270
  349.7 1.9 copy.269
  353.4 2.4 pad_maximum_fusion.3
  360.6 1.9 fusion.181
  362.5 24.5 %all-reduce.19.cloned.1.call-done = (bf16[1,64,6,128]{3,1,0,2:T(8,128)(2,1)}, bf16[1,64,6,128]{3,1,2,0:T(8,128)(2,1)}) async-done(((bf16[1,64,6,128]{3,1,0,2:T(8,128)(2,1)}, bf16[1,64,6,128]{3,1,2,0:T(8,128)(2,1)}), (bf16[1,64,6,128]{3,1,0,2:T(8,128)(2,1)}, bf16[1,64,6,128]{3,1,2,0:T(8,128)(2,1)})) %all-reduce.19.cloned.1.call-update) | async-done | bytes 196624 | tf_op jit(solution)/shard_map/psum | solution.py:19
  387.0 3.2 fusion.189
  390.2 38.0 %all-gather.8.cloned.1.call-done = f32[8,792,64]{1,2,0:T(8,128)} async-done(((f32[1,792,64]{1,2,0:T(8,128)}), f32[8,792,64]{1,2,0:T(8,128)}) %all-gather.8.cloned.1.call-update) | async-done | bytes 1622032 | tf_op jit(solution)/shard_map/all_gather | solution.py:48
  433.3 11.9 %all-gather.5 = f32[4,792,64]{1,2,0:T(8,128)S(1)} all-gather(f32[1,792,64]{1,2,0:T(8,128)S(1)} %maximum_bitcast_fusion.2), channel_id=4, replica_groups=mesh['seq_0'=4,'seq_1'=8,'seq_2'=4,'mp'=2] {'seq_2'}, dimensions={0}, use_global_device_ids=true | all-gather | bytes 1013760 | tf_op jit(solution)/shard_map/all_gather | solution.py:48
  446.0 1.9 squeeze.257
  447.9 1.9 squeeze.255
  449.9 1.9 squeeze.253
  453.7 3.7 fusion.34
  457.4 3.1 gather_fusion.1
  469.4 12.9 %all_to_all.27 = f32[2,256,768]{2,1,0:T(8,128)} all-to-all(f32[2,256,768]{2,1,0:T(8,128)S(1)} %broadcast_in_dim.24), channel_id=1, replica_groups=mesh['seq_0'=4,'seq_1'=8,'seq_2'=4,'mp'=2] {'mp'}, dimensions={0} | all-to-all | bytes 3145728 | tf_op jit(solution)/shard_map/all_to_all | solution.py:68
  485.1 6.2 %fusion.24 = f32[256,768]{1,0:T(8,128)S(1)} fusion(bf16[1536,768]{1,0:T(8,128)(2,1)S(1)} %copy-done, bf16[256,768]{1,0:T(8,128)(2,1)S(1)} %multiply_convert_fusion.1, bf16[768,1536]{1,0:T(8,128)(2,1)} %param.13), kind=kOutput, calls=%fused_computation.56 | convolution fusion | flops 1233518592 | bytes 5898240 | tf_op jit(solution)/shard_map/dot_general | solution.py:271
  491.5 5.7 %all_to_all.28 = f32[2,256,768]{2,1,0:T(8,128)} all-to-all(f32[2,256,768]{2,1,0:T(8,128)S(1)} %broadcast_in_dim.25), channel_id=1, replica_groups=mesh['seq_0'=4,'seq_1'=8,'seq_2'=4,'mp'=2] {'mp'}, dimensions={0} | all-to-all | bytes 3145728 | tf_op jit(solution)/shard_map/all_to_all | solution.py:68
  (225 shorter events, 56.4 us)
Async XLA Ops:
  6.5 478.6 %copy-start = (bf16[1536,768]{1,0:T(8,128)(2,1)S(1)}, bf16[1536,768]{1,0:T(8,128)(2,1)}, u32[]{:S(2)}) copy-start(bf16[1536,768]{1,0:T(8,128)(2,1)} %param.14) | copy-start | bytes 7077892
  9.9 21.9 %copy-start.26 = (s32[72]{0:T(128)}, s32[72]{0:T(128)S(1)}, u32[]{:S(2)}) copy-start(s32[72]{0:T(128)S(1)} %fusion.141) | copy-start | bytes 868
  11.5 73.7 %all-to-all-start = ((s32[128,1,2]{2,1,0:T(1,128)}), s32[128,1,2]{2,1,0:T(1,128)}, u32[]{:S(2)}, u32[]{:S(2)}) async-start(s32[128,1,2]{2,1,0:T(1,128)} %bitcast.15), calls=%async_computation | async-start | bytes 131072 | tf_op jit(solution)/shard_map/all_to_all | solution.py:190
  28.4 55.6 %all-reduce.21.cloned.1.call-start = ((), (), s32[]{:S(2)}) async-start(), calls=%async_computation.9 | async-start | bytes 393216 | tf_op jit(solution)/shard_map/psum | solution.py:19
  32.5 5.7 %copy-start.7 = (bf16[256,768]{1,0:T(8,128)(2,1)S(1)}, bf16[256,768]{1,0:T(8,128)(2,1)}, u32[]{:S(2)}) copy-start(bf16[256,768]{1,0:T(8,128)(2,1)} %param.10) | copy-start | bytes 1179652
  34.4 7.9 %copy-start.5 = (bf16[4,64,6,64]{1,0,3,2:T(4,128)(2,1)}, bf16[4,64,6,64]{1,0,3,2:T(4,128)(2,1)S(1)}, u32[]{:S(2)}) copy-start(bf16[4,64,6,64]{1,0,3,2:T(4,128)(2,1)S(1)} %reshape.908) | copy-start | bytes 589828
  36.0 6.4 %copy-start.11 = (bf16[4,64,6,64]{3,1,2,0:T(8,128)(2,1)}, bf16[4,64,6,64]{3,1,2,0:T(8,128)(2,1)S(1)}, u32[]{:S(2)}) copy-start(bf16[4,64,6,64]{3,1,2,0:T(8,128)(2,1)S(1)} %copy.275) | copy-start | bytes 589828
  38.1 118.3 %all-reduce.13.cloned.1.call-start = ((), (), s32[]{:S(2)}) async-start(), calls=%async_computation.5 | async-start | bytes 393216 | tf_op jit(solution)/shard_map/psum | solution.py:19
  84.0 128.5 %all-reduce.23.cloned.1.call-start = ((), (), s32[]{:S(2)}) async-start(), calls=%async_computation.10 | async-start | bytes 393216 | tf_op jit(solution)/shard_map/psum | solution.py:19
  84.9 179.6 %all-reduce.17.cloned.1.call-start = ((), (), s32[]{:S(2)}) async-start(), calls=%async_computation.7 | async-start | bytes 393216 | tf_op jit(solution)/shard_map/psum | solution.py:19
  159.5 12.3 %copy-start.13 = (bf16[256,384]{1,0:T(8,128)(2,1)S(1)}, bf16[256,384]{1,0:T(8,128)(2,1)}, u32[]{:S(2)}) copy-start(bf16[256,384]{1,0:T(8,128)(2,1)} %convolution_convert_fusion.2) | copy-start | bytes 589828
  159.5 12.5 %copy-start.15 = (bf16[256,384]{1,0:T(8,128)(2,1)S(1)}, bf16[256,384]{1,0:T(8,128)(2,1)}, u32[]{:S(2)}) copy-start(bf16[256,384]{1,0:T(8,128)(2,1)} %convolution_convert_fusion.1) | copy-start | bytes 589828
  159.5 297.9 %all-to-all-start.1 = ((bf16[128,2,64,128]{3,2,1,0:T(8,128)(2,1)}), bf16[128,2,64,128]{3,2,1,0:T(8,128)(2,1)}, u32[]{:S(2)}, u32[]{:S(2)}) async-start(bf16[128,2,64,128]{3,2,1,0:T(8,128)(2,1)} %bitcast.514), calls=%async_computation.1 | async-start | bytes 8388608 | tf_op jit(solution)/shard_map/all_to_all | solution.py:189
  171.8 164.2 %all-reduce.15.cloned.1.call-start = ((), (), s32[]{:S(2)}) async-start(), calls=%async_computation.6 | async-start | bytes 393216 | tf_op jit(solution)/shard_map/psum | solution.py:19
  212.5 174.5 %all-reduce.19.cloned.1.call-start = ((), (), s32[]{:S(2)}) async-start(), calls=%async_computation.8 | async-start | bytes 393216 | tf_op jit(solution)/shard_map/psum | solution.py:19
  336.0 92.2 %all-gather.8.cloned.1.call-start = ((), (), s32[]{:S(2)}) async-start(), calls=%async_computation.4 | async-start | bytes 2064384 | tf_op jit(solution)/shard_map/all_gather | solution.py:48
  336.2 8.9 %copy-start.16 = (bf16[256,384]{1,0:T(8,128)(2,1)S(1)}, bf16[256,384]{1,0:T(8,128)(2,1)}, u32[]{:S(2)}) copy-start(bf16[256,384]{1,0:T(8,128)(2,1)} %convolution_convert_fusion.1) | copy-start | bytes 589828
  336.2 10.0 %copy-start.14 = (bf16[256,384]{1,0:T(8,128)(2,1)S(1)}, bf16[256,384]{1,0:T(8,128)(2,1)}, u32[]{:S(2)}) copy-start(bf16[256,384]{1,0:T(8,128)(2,1)} %convolution_convert_fusion.2) | copy-start | bytes 589828
  336.2 11.1 %copy-start.6 = (bf16[4,64,6,64]{1,0,3,2:T(4,128)(2,1)S(1)}, bf16[4,64,6,64]{1,0,3,2:T(4,128)(2,1)}, u32[]{:S(2)}) copy-start(bf16[4,64,6,64]{1,0,3,2:T(4,128)(2,1)} %copy-done.5) | copy-start | bytes 589828
  339.8 13.6 %collective-permute-start = (bf16[64,6,128]{0,2,1:T(8,128)(2,1)}, bf16[64,6,128]{0,2,1:T(8,128)(2,1)}, u32[]{:S(2)}, u32[]{:S(2)}) collective-permute-start(bf16[64,6,128]{0,2,1:T(8,128)(2,1)} %get-tuple-element.74), channel_id=1, source_target_pairs={{0,2},{2,4},{4,6},{6,8},{8,10},{10,12},{12,14},{14,16},{16,18},{18... | collective-permute-start | bytes 294920 | tf_op jit(solution)/shard_map/ppermute | solution.py:31
  343.6 9.9 %collective-permute-start.1 = (bf16[64,6,128]{0,2,1:T(8,128)(2,1)}, bf16[64,6,128]{0,2,1:T(8,128)(2,1)}, u32[]{:S(2)}, u32[]{:S(2)}) collective-permute-start(bf16[64,6,128]{0,2,1:T(8,128)(2,1)} %get-tuple-element.75), channel_id=1, source_target_pairs={{2,0},{4,2},{6,4},{8,6},{10,8},{12,10},{14,12},{16,14},{18,16},{20... | collective-permute-start | bytes 294920 | tf_op jit(solution)/shard_map/ppermute | solution.py:33
  346.2 5.4 %copy-start.28 = (s32[2]{0:T(128)S(1)}, s32[2]{0:T(128)}, u32[]{:S(2)}) copy-start(s32[2]{0:T(128)} %param.17) | copy-start | bytes 28
  346.2 6.6 %copy-start.27 = (s32[72]{0:T(128)S(1)}, s32[72]{0:T(128)}, u32[]{:S(2)}) copy-start(s32[72]{0:T(128)} %copy-done.26) | copy-start | bytes 868
  347.6 39.4 %copy-start.10 = (bf16[4,64,6,64,1]{3,1,4,2,0:T(8,128)(2,1)}, bf16[4,64,6,64,1]{3,1,4,2,0:T(8,128)(2,1)S(1)}, u32[]{:S(2)}) copy-start(bf16[4,64,6,64,1]{3,1,4,2,0:T(8,128)(2,1)S(1)} %copy.333) | copy-start | bytes 589828
  351.6 4.2 copy-start.29
  358.0 1.6 copy-start.12
  460.5 1.6 copy-start.21
  460.5 1.8 copy-start.1
  460.5 2.2 copy-start.2
  465.4 1.3 copy-start.4
  466.6 1.2 copy-start.24
  482.3 1.6 copy-start.8
  (9 other events, 9.3 us)
Sparse Core Ops, SparseCore 0:
  38.2 45.6 all-reduce.20
  86.5 69.8 all-reduce.12
  158.7 53.7 all-reduce.22
  214.8 49.6 all-reduce.16
  266.7 69.2 all-reduce.14
  338.3 48.6 all-reduce.18
  388.8 39.4 all-gather.7
where the time goes:
time: 509 us; the launch traced here: 507 us
  waiting for transfers between devices  310 us (61%)
  local copies, waits for them, and re-layouts  45.3 us (9%)
  blocking collectives  43.1 us (8%)
  starting transfers between devices  34.7 us (7%)
  matrix products  27.7 us (5%)
  other arithmetic  27.3 us (5%)
  between operations  19.6 us (4%)
    psum x6, waiting for transfers between devices, from_root(): value = lax.psum(value, axis)  271 us
    all_gather x1, waiting for transfers between devices, collected_together(): both, at, found = (lax.all_gather(jnp.concatenate(lines), axis), 0, {})  38 us
    all_gather x2, blocking collectives, collected_together(): both, at, found = (lax.all_gather(jnp.concatenate(lines), axis), 0, {})  24.5 us
    all_to_all x2, blocking collectives, from_everyone(): return lax.all_to_all(copies, axis, split_axis=0, concat_axis=0, tiled=True)  18.6 us
    all_to_all x1, starting transfers between devices, shards(): lax.all_to_all(wanted, SEQ, split_axis=0, concat_axis=0, tiled=True)  16.9 us
    concatenate x8, local copies, waits for them, and re-layouts, shards(): jnp.concatenate([key_part.reshape(tokens_here, head_count, HD), value_par...  12.6 us
    all_to_all x1, starting transfers between devices, shards(): lax.all_to_all(block_table[lax.all_to_all(wanted, SEQ, split_axis=0, conc...  12.3 us
  transfers between devices with their start and end apart: 11, of which 7 were waited for; matrix products, arithmetic and copies ran while one was open for 14% of the time, Pallas kernels for 0%

commit v1 on v0

--- a/solution.py
+++ b/solution.py
@@ -16,7 +16,7 @@
 def from_root(value, axes, root):
     value = jnp.where(lax.axis_index(axes) == root, value, jnp.zeros_like(value))
     for axis in axes:
-        value = lax.psum(value, axis)
+        value = jnp.sum(lax.all_gather(value, axis), axis=0)
     return value
 
 

time: 509 us -> 461 us (0.906)
  waiting for transfers between devices: 310 us -> 0.03 us
  blocking collectives: 43.1 us -> 295 us
  other arithmetic: 27.3 us -> 37.3 us
  local copies, waits for them, and re-layouts: 45.3 us -> 50.6 us
    psum x6 -> x0, waiting for transfers between devices: 271 us -> none  [from_root(): value = lax.psum(value, axis)]
    all_gather x0 -> x12, blocking collectives: none -> 204 us  [from_root(): value = jnp.sum(lax.all_gather(value, axis), axis=0)]
    all_to_all x2, blocking collectives: 18.6 us -> 64.5 us  [from_everyone(): return lax.all_to_all(copies, axis, split_axis=0, concat_axis=0, tiled=True)]
    all_gather x1, waiting for transfers between devices: 38 us -> 0.01 us  [collected_together(): both, at, found = (lax.all_gather(jnp.concatenate(lines), axis), 0, {})]
    reduce_sum x0 -> x12, other arithmetic: none -> 8.98 us  [from_root(): value = jnp.sum(lax.all_gather(value, axis), axis=0)]
    concatenate x8 -> x7, local copies, waits for them, and re-layouts: 12.6 us -> 11 us  [shards(): jnp.concatenate([key_part.reshape(tokens_here, head_count, HD), value_par...]
  transfers between devices with their start and end apart: 11 -> 5, of which waited for: 7 -> 0; matrix products, arithmetic and copies ran while one was open for 14% -> 18% of each run, Pallas kernels for 0% -> 0%
where the time goes in v1:
time: 461 us; the launch traced here: 460 us
  blocking collectives  295 us (64%)
  local copies, waits for them, and re-layouts  50.6 us (11%)
  other arithmetic  37.3 us (8%)
  starting transfers between devices  32.8 us (7%)
  matrix products  24.9 us (5%)
  between operations  19.2 us (4%)
    all_gather x12, blocking collectives, from_root(): value = jnp.sum(lax.all_gather(value, axis), axis=0)  204 us
    all_to_all x2, blocking collectives, from_everyone(): return lax.all_to_all(copies, axis, split_axis=0, concat_axis=0, tiled=True)  64.5 us
    all_gather x2, blocking collectives, collected_together(): both, at, found = (lax.all_gather(jnp.concatenate(lines), axis), 0, {})  26.5 us
    all_to_all x1, starting transfers between devices, shards(): lax.all_to_all(wanted, SEQ, split_axis=0, concat_axis=0, tiled=True)  16.9 us
    all_to_all x1, starting transfers between devices, shards(): lax.all_to_all(block_table[lax.all_to_all(wanted, SEQ, split_axis=0, conc...  11.5 us
    concatenate x7, local copies, waits for them, and re-layouts, shards(): jnp.concatenate([key_part.reshape(tokens_here, head_count, HD), value_par...  11 us
  transfers between devices with their start and end apart: 5, of which 0 were waited for; matrix products, arithmetic and copies ran while one was open for 18% of the time, Pallas kernels for 0%

profile of v1, /device:TPU:1, one launch (start us, length us, event | category | flops | bytes accessed | tf_op | source)
XLA Modules:
  0.0 459.5 jit_solution(5131605182700496279)
XLA Ops:
  11.5 16.9 %all-to-all-start = ((s32[128,1,2]{2,1,0:T(1,128)}), s32[128,1,2]{2,1,0:T(1,128)}, u32[]{:S(2)}, u32[]{:S(2)}) async-start(s32[128,1,2]{2,1,0:T(1,128)} %bitcast.15), calls=%async_computation | async-start | bytes 131072 | tf_op jit(solution)/shard_map/all_to_all | solution.py:190
  32.6 3.1 collective-permute-start
  47.9 14.7 %all_gather.97 = bf16[4,64,6,64]{3,1,2,0:T(8,128)(2,1)S(1)} all-gather(bf16[1,64,6,64]{3,1,2,0:T(8,128)(2,1)S(1)} %copy.311), channel_id=1, replica_groups=mesh['seq_0'=4,'seq_1'=8,'seq_2'=4,'mp'=2] {'seq_0'}, dimensions={0}, use_global_device_ids=true | all-gather | bytes 245760 | tf_op jit(solution)/shard_map/all_gather | solution.py:19
  63.4 19.9 %all-gather.6 = bf16[512,6,64]{2,0,1:T(8,128)(2,1)S(1)} all-gather(bf16[64,6,64]{2,0,1:T(8,128)(2,1)} %reduce_sum.249), channel_id=8, replica_groups=mesh['seq_0'=4,'seq_1'=8,'seq_2'=4,'mp'=2] {'seq_1'}, dimensions={0}, use_global_device_ids=true | all-gather | bytes 442368 | tf_op jit(solution)/shard_map/all_gather | solution.py:19
  84.1 10.4 %all-gather.7 = bf16[256,6,64]{2,0,1:T(8,128)(2,1)S(1)} all-gather(bf16[64,6,64]{2,0,1:T(8,128)(2,1)} %reduce_sum.250), channel_id=9, replica_groups=mesh['seq_0'=4,'seq_1'=8,'seq_2'=4,'mp'=2] {'seq_2'}, dimensions={0}, use_global_device_ids=true | all-gather | bytes 245760 | tf_op jit(solution)/shard_map/all_gather | solution.py:19
  96.4 10.2 %all_gather.92 = bf16[4,64,6,64]{3,1,2,0:T(8,128)(2,1)S(1)} all-gather(bf16[1,64,6,64]{3,1,2,0:T(8,128)(2,1)S(1)} %copy.308), channel_id=1, replica_groups=mesh['seq_0'=4,'seq_1'=8,'seq_2'=4,'mp'=2] {'seq_0'}, dimensions={0}, use_global_device_ids=true | all-gather | bytes 245760 | tf_op jit(solution)/shard_map/all_gather | solution.py:19
  107.3 19.9 %all-gather.4 = bf16[512,6,64]{2,0,1:T(8,128)(2,1)S(1)} all-gather(bf16[64,6,64]{2,0,1:T(8,128)(2,1)} %reduce_sum.246), channel_id=6, replica_groups=mesh['seq_0'=4,'seq_1'=8,'seq_2'=4,'mp'=2] {'seq_1'}, dimensions={0}, use_global_device_ids=true | all-gather | bytes 442368 | tf_op jit(solution)/shard_map/all_gather | solution.py:19
  128.1 9.9 %all-gather.5 = bf16[256,6,64]{2,0,1:T(8,128)(2,1)S(1)} all-gather(bf16[64,6,64]{2,0,1:T(8,128)(2,1)} %reduce_sum.247), channel_id=7, replica_groups=mesh['seq_0'=4,'seq_1'=8,'seq_2'=4,'mp'=2] {'seq_2'}, dimensions={0}, use_global_device_ids=true | all-gather | bytes 245760 | tf_op jit(solution)/shard_map/all_gather | solution.py:19
  144.4 2.3 fusion.27
  153.0 3.1 gather_fusion
  156.1 11.5 %all-to-all-start.1 = ((bf16[128,2,64,128]{3,2,1,0:T(8,128)(2,1)}), bf16[128,2,64,128]{3,2,1,0:T(8,128)(2,1)}, u32[]{:S(2)}, u32[]{:S(2)}) async-start(bf16[128,2,64,128]{3,2,1,0:T(8,128)(2,1)} %bitcast.514), calls=%async_computation.1 | async-start | bytes 8388608 | tf_op jit(solution)/shard_map/all_to_all | solution.py:189
  167.6 15.3 %all-gather.11 = f32[4,792,64]{1,2,0:T(8,128)S(1)} all-gather(f32[1,792,64]{1,2,0:T(8,128)S(1)} %maximum_bitcast_fusion), channel_id=10, replica_groups=mesh['seq_0'=4,'seq_1'=8,'seq_2'=4,'mp'=2] {'seq_0'}, dimensions={0}, use_global_device_ids=true | all-gather | bytes 1013760 | tf_op jit(solution)/shard_map/all_gather | solution.py:48
  187.8 2.1 reshape.963
  189.8 2.0 reshape.962
  195.9 13.9 %all_gather.87 = bf16[4,64,6,128]{3,1,2,0:T(8,128)(2,1)S(1)} all-gather(bf16[1,64,6,128]{3,1,2,0:T(8,128)(2,1)S(1)} %copy.297), channel_id=1, replica_groups=mesh['seq_0'=4,'seq_1'=8,'seq_2'=4,'mp'=2] {'seq_0'}, dimensions={0}, use_global_device_ids=true | all-gather | bytes 491520 | tf_op jit(solution)/shard_map/all_gather | solution.py:19
  210.6 48.3 %all-gather.2 = bf16[512,6,128]{2,0,1:T(8,128)(2,1)S(1)} all-gather(bf16[64,6,128]{2,0,1:T(8,128)(2,1)} %reduce_sum.241), channel_id=4, replica_groups=mesh['seq_0'=4,'seq_1'=8,'seq_2'=4,'mp'=2] {'seq_1'}, dimensions={0}, use_global_device_ids=true | all-gather | bytes 884736 | tf_op jit(solution)/shard_map/all_gather | solution.py:19
  259.7 14.9 %all-gather.3 = bf16[256,6,128]{2,0,1:T(8,128)(2,1)S(1)} all-gather(bf16[64,6,128]{2,0,1:T(8,128)(2,1)} %reduce_sum.242), channel_id=5, replica_groups=mesh['seq_0'=4,'seq_1'=8,'seq_2'=4,'mp'=2] {'seq_2'}, dimensions={0}, use_global_device_ids=true | all-gather | bytes 491520 | tf_op jit(solution)/shard_map/all_gather | solution.py:19
  276.5 10.7 %all_gather.82 = bf16[4,64,6,128]{3,1,2,0:T(8,128)(2,1)S(1)} all-gather(bf16[1,64,6,128]{3,1,2,0:T(8,128)(2,1)S(1)} %copy.294), channel_id=1, replica_groups=mesh['seq_0'=4,'seq_1'=8,'seq_2'=4,'mp'=2] {'seq_0'}, dimensions={0}, use_global_device_ids=true | all-gather | bytes 491520 | tf_op jit(solution)/shard_map/all_gather | solution.py:19
  287.9 20.4 %all-gather = bf16[512,6,128]{2,0,1:T(8,128)(2,1)S(1)} all-gather(bf16[64,6,128]{2,0,1:T(8,128)(2,1)} %reduce_sum.238), channel_id=2, replica_groups=mesh['seq_0'=4,'seq_1'=8,'seq_2'=4,'mp'=2] {'seq_1'}, dimensions={0}, use_global_device_ids=true | all-gather | bytes 884736 | tf_op jit(solution)/shard_map/all_gather | solution.py:19
  309.0 10.4 %all-gather.1 = bf16[256,6,128]{2,0,1:T(8,128)(2,1)S(1)} all-gather(bf16[64,6,128]{2,0,1:T(8,128)(2,1)} %reduce_sum.239), channel_id=3, replica_groups=mesh['seq_0'=4,'seq_1'=8,'seq_2'=4,'mp'=2] {'seq_2'}, dimensions={0}, use_global_device_ids=true | all-gather | bytes 491520 | tf_op jit(solution)/shard_map/all_gather | solution.py:19
  320.2 1.9 copy.280
  322.1 1.9 copy.279
  332.7 2.4 fusion.177
  340.3 11.2 %all-gather.13 = f32[4,792,64]{1,2,0:T(8,128)S(1)} all-gather(f32[1,792,64]{1,2,0:T(8,128)S(1)} %maximum_bitcast_fusion.2), channel_id=12, replica_groups=mesh['seq_0'=4,'seq_1'=8,'seq_2'=4,'mp'=2] {'seq_2'}, dimensions={0}, use_global_device_ids=true | all-gather | bytes 1013760 | tf_op jit(solution)/shard_map/all_gather | solution.py:48
  352.3 2.0 squeeze.257
  354.2 1.9 squeeze.255
  356.2 1.9 squeeze.253
  360.0 3.7 fusion.34
  363.7 3.1 gather_fusion.1
  375.8 58.8 %all_to_all.27 = f32[2,256,768]{2,1,0:T(8,128)} all-to-all(f32[2,256,768]{2,1,0:T(8,128)S(1)} %broadcast_in_dim.24), channel_id=1, replica_groups=mesh['seq_0'=4,'seq_1'=8,'seq_2'=4,'mp'=2] {'mp'}, dimensions={0} | all-to-all | bytes 3145728 | tf_op jit(solution)/shard_map/all_to_all | solution.py:68
  437.4 6.2 %fusion.24 = f32[256,768]{1,0:T(8,128)S(1)} fusion(bf16[1536,768]{1,0:T(8,128)(2,1)S(1)} %copy-done, bf16[256,768]{1,0:T(8,128)(2,1)S(1)} %multiply_convert_fusion.1, bf16[768,1536]{1,0:T(8,128)(2,1)} %param.13), kind=kOutput, calls=%fused_computation.56 | convolution fusion | flops 1233518592 | bytes 5898240 | tf_op jit(solution)/shard_map/dot_general | solution.py:271
  443.8 5.7 %all_to_all.28 = f32[2,256,768]{2,1,0:T(8,128)} all-to-all(f32[2,256,768]{2,1,0:T(8,128)S(1)} %broadcast_in_dim.25), channel_id=1, replica_groups=mesh['seq_0'=4,'seq_1'=8,'seq_2'=4,'mp'=2] {'mp'}, dimensions={0} | all-to-all | bytes 3145728 | tf_op jit(solution)/shard_map/all_to_all | solution.py:68
  (240 shorter events, 79.6 us)
Async XLA Ops:
  6.5 430.9 %copy-start = (bf16[1536,768]{1,0:T(8,128)(2,1)S(1)}, bf16[1536,768]{1,0:T(8,128)(2,1)}, u32[]{:S(2)}) copy-start(bf16[1536,768]{1,0:T(8,128)(2,1)} %param.14) | copy-start | bytes 7077892
  6.5 23.4 %copy-start.11 = (bf16[256,768]{1,0:T(8,128)(2,1)S(1)}, bf16[256,768]{1,0:T(8,128)(2,1)}, u32[]{:S(2)}) copy-start(bf16[256,768]{1,0:T(8,128)(2,1)} %param.10) | copy-start | bytes 1179652
  9.9 1.6 copy-start.28
  11.5 140.5 %all-to-all-start = ((s32[128,1,2]{2,1,0:T(1,128)}), s32[128,1,2]{2,1,0:T(1,128)}, u32[]{:S(2)}, u32[]{:S(2)}) async-start(s32[128,1,2]{2,1,0:T(1,128)} %bitcast.15), calls=%async_computation | async-start | bytes 131072 | tf_op jit(solution)/shard_map/all_to_all | solution.py:190
  29.9 1.5 copy-start.19
  31.5 7.2 %copy-start.20 = (bf16[256,384]{1,0:T(8,128)(2,1)}, bf16[256,384]{1,0:T(8,128)(2,1)S(1)}, u32[]{:S(2)}) copy-start(bf16[256,384]{1,0:T(8,128)(2,1)S(1)} %convolution_convert_fusion.1) | copy-start | bytes 589828
  31.6 8.0 %copy-start.6 = (bf16[256,384]{0,1:T(8,128)(2,1)}, bf16[256,384]{0,1:T(8,128)(2,1)S(1)}, u32[]{:S(2)}) copy-start(bf16[256,384]{0,1:T(8,128)(2,1)S(1)} %copy.274) | copy-start | bytes 589828
  31.8 7.8 %copy-start.8 = (bf16[256,384]{0,1:T(8,128)(2,1)}, bf16[256,384]{0,1:T(8,128)(2,1)S(1)}, u32[]{:S(2)}) copy-start(bf16[256,384]{0,1:T(8,128)(2,1)S(1)} %copy.275) | copy-start | bytes 589828
  31.8 7.8 %copy-start.30 = (s32[2]{0:T(128)S(1)}, s32[2]{0:T(128)}, u32[]{:S(2)}) copy-start(s32[2]{0:T(128)} %param.17) | copy-start | bytes 28
  32.6 295.0 %collective-permute-start = (bf16[64,6,128]{0,2,1:T(8,128)(2,1)}, bf16[64,6,128]{0,2,1:T(8,128)(2,1)}, u32[]{:S(2)}, u32[]{:S(2)}) collective-permute-start(bf16[64,6,128]{0,2,1:T(8,128)(2,1)} %get-tuple-element.62), channel_id=1, source_target_pairs={{0,2},{2,4},{4,6},{6,8},{8,10},{10,12},{12,14},{14,16},{16,18},{18... | collective-permute-start | bytes 294920 | tf_op jit(solution)/shard_map/ppermute | solution.py:31
  35.7 291.9 %collective-permute-start.1 = (bf16[64,6,128]{0,2,1:T(8,128)(2,1)}, bf16[64,6,128]{0,2,1:T(8,128)(2,1)}, u32[]{:S(2)}, u32[]{:S(2)}) collective-permute-start(bf16[64,6,128]{0,2,1:T(8,128)(2,1)} %get-tuple-element.63), channel_id=1, source_target_pairs={{2,0},{4,2},{6,4},{8,6},{10,8},{12,10},{14,12},{16,14},{18,16},{20... | collective-permute-start | bytes 294920 | tf_op jit(solution)/shard_map/ppermute | solution.py:33
  156.1 207.6 %all-to-all-start.1 = ((bf16[128,2,64,128]{3,2,1,0:T(8,128)(2,1)}), bf16[128,2,64,128]{3,2,1,0:T(8,128)(2,1)}, u32[]{:S(2)}, u32[]{:S(2)}) async-start(bf16[128,2,64,128]{3,2,1,0:T(8,128)(2,1)} %bitcast.514), calls=%async_computation.1 | async-start | bytes 8388608 | tf_op jit(solution)/shard_map/all_to_all | solution.py:189
  167.6 167.5 %all-gather.16.cloned.1.call-start = ((), (), s32[]{:S(2)}) async-start(), calls=%async_computation.4 | async-start | bytes 2064384 | tf_op jit(solution)/shard_map/all_gather | solution.py:48
  187.0 5.9 %copy-start.5 = (bf16[4,64,6,128]{1,0,3,2:T(4,128)(2,1)S(1)}, bf16[4,64,6,128]{1,0,3,2:T(4,128)(2,1)}, u32[]{:S(2)}) copy-start(bf16[4,64,6,128]{1,0,3,2:T(4,128)(2,1)} %constant_dynamic-update-slice_fusion) | copy-start | bytes 1179652
  309.0 15.0 %copy-start.31 = (s32[2]{0:T(128)S(1)}, s32[2]{0:T(128)}, u32[]{:S(2)}) copy-start(s32[2]{0:T(128)} %param.17) | copy-start | bytes 28
  309.0 16.2 %copy-start.14 = (bf16[4,64,6,64,1]{3,1,4,2,0:T(8,128)(2,1)S(1)}, bf16[4,64,6,64,1]{3,1,4,2,0:T(8,128)(2,1)}, u32[]{:S(2)}) copy-start(bf16[4,64,6,64,1]{3,1,4,2,0:T(8,128)(2,1)} %copy.350) | copy-start | bytes 589828
  320.2 5.1 %copy-start.15 = (bf16[64,6,128]{2,0,1:T(8,128)(2,1)S(1)}, bf16[64,6,128]{2,0,1:T(8,128)(2,1)}, u32[]{:S(2)}) copy-start(bf16[64,6,128]{2,0,1:T(8,128)(2,1)} %reduce_sum.243) | copy-start | bytes 294916
  320.2 5.1 %copy-start.17 = (bf16[64,6,128]{2,0,1:T(8,128)(2,1)S(1)}, bf16[64,6,128]{2,0,1:T(8,128)(2,1)}, u32[]{:S(2)}) copy-start(bf16[64,6,128]{2,0,1:T(8,128)(2,1)} %reduce_sum.240) | copy-start | bytes 294916
  322.1 4.9 %copy-start.29 = (s32[72]{0:T(128)S(1)}, s32[72]{0:T(128)}, u32[]{:S(2)}) copy-start(s32[72]{0:T(128)} %copy-done.28) | copy-start | bytes 868
  322.1 5.5 %copy-start.7 = (bf16[256,384]{0,1:T(8,128)(2,1)S(1)}, bf16[256,384]{0,1:T(8,128)(2,1)}, u32[]{:S(2)}) copy-start(bf16[256,384]{0,1:T(8,128)(2,1)} %copy-done.6) | copy-start | bytes 589828
  322.1 5.5 %copy-start.9 = (bf16[256,384]{0,1:T(8,128)(2,1)S(1)}, bf16[256,384]{0,1:T(8,128)(2,1)}, u32[]{:S(2)}) copy-start(bf16[256,384]{0,1:T(8,128)(2,1)} %copy-done.8) | copy-start | bytes 589828
  324.0 3.6 copy-start.32
  366.8 1.7 copy-start.23
  366.8 1.8 copy-start.1
  366.8 2.2 copy-start.2
  371.6 1.3 copy-start.4
  372.9 1.1 copy-start.16
  372.9 1.1 copy-start.18
  372.9 1.2 copy-start.21
  372.9 1.2 copy-start.26
  374.2 1.1 copy-start.22
  434.6 1.6 copy-start.12
  (6 other events, 5.6 us)
Sparse Core Ops, SparseCore 0:
  187.9 88.2 all-gather.15
